TPU v7x, 256 devices: a whole 4x4x8 slice. The times are simulated.
256 devices in a mesh: doc: 32 (over y, x, core), term: 4 (over z_lo), pair: 2 (over z_hi).
Axes of the slice: x: 4, y: 4, z: 8 (z_hi: 2, z_lo: 4; z = z_hi * 4 + z_lo), core: 2. Of those that a mesh axis runs over, the one named last changes fastest.
Arguments:
- counts: int32 [64, 16, 128, 128], P('doc', 'term'), may hold values from 0 to 11
- block_ids: int32 [64, 16], P('doc', 'term'), may hold values from 0 to 8191, as said below
- live_slots: int32 [64, 16], P('doc', 'term'), may hold values 0 or 1
- lengths: int32 [8192], P('doc'), may hold values from 1 to 24528, as said below
- pairs: int32 [4096, 2], P(('doc', 'pair')), may hold values from 0 to 63, as said below
- pair_count: int32 [64], P(('doc', 'pair')), may hold values from 1 to 64, as said below
Outputs:
- gram: float32 [4096, 128, 128], P(('doc', 'pair'), 'term')
Inputs may be any that keep to these rules, and one draw needn't show every extreme that they name: `block_ids`: columns s * 4 to (s + 1) * 4 - 1 hold term blocks of the s-th of 4 equal ranges of the 8192 blocks, distinct within one document block and range. `lengths`: document b * 128 + r has a length of the sum of counts[b, s, r, t] over all slots s and all t plus tokens outside its blocks: 1 to 2000 of them for every document but the last, whose length is exactly 24528. `pairs`: the left block of row k belongs to doc index k // 128. Rows k with k % 64 < pair_count[k // 64] are live; some entry equals 64.
All inputs are finite; a program needn't handle non-finite values. No bound on the sum of `live_slots` on one device may be relied on, other than what follows from the above.
Results may differ from a plain program's by a relative error of at most 0.0014.
Values may be sent and summed in bfloat16 or wider, within the bound.
No kernel may reach another device: no remote copies, remote signals or barrier semaphores. Data moves between devices by JAX's collectives and lax.ppermute only.
A program may use at most 64 MiB of HBM per device.

v0:
```python
import jax
import jax.numpy as jnp
from jax import lax
from jax.sharding import PartitionSpec as P

V = 1048576
PB = 8
saturation = 1.2
length_weight = 0.75
epsilon = 1e-06


def gram_block(normalized, block_ids, whole_tiles, whole_ids, pair_batch, left_base):
    left_index = pair_batch[:, 0] - left_base
    right_pair_index = pair_batch[:, 1]
    left_tiles = normalized[left_index]
    right_tiles = whole_tiles[right_pair_index]
    matches = (block_ids[left_index][:, :, None] == whole_ids[right_pair_index][:, None, :]).astype(
        jnp.bfloat16
    )
    aligned = jnp.einsum(
        "pij,pjet->piet", matches, right_tiles, preferred_element_type=jnp.float32
    ).astype(jnp.bfloat16)
    return jnp.einsum("pidt,piet->pde", left_tiles, aligned, preferred_element_type=jnp.float32)


def run_pairs(work_pairs, work_count, normalized, block_ids, whole_tiles, whole_ids, left_base):
    capacity = work_pairs.shape[0]
    doc_rows = normalized.shape[2]
    step_count = (work_count + PB - 1) // PB

    def pair_step(loop_index, partial_value):
        first_row = loop_index * PB
        pair_batch = lax.dynamic_slice_in_dim(work_pairs, first_row, PB, 0)
        gram_tiles = gram_block(
            normalized, block_ids, whole_tiles, whole_ids, pair_batch, left_base
        )
        live_mask = first_row + jnp.arange(PB, dtype=jnp.int32) < work_count
        gram_tiles = jnp.where(live_mask[:, None, None], gram_tiles, 0.0)
        return lax.dynamic_update_slice_in_dim(partial_value, gram_tiles, first_row, 0)

    return lax.fori_loop(
        0, step_count, pair_step, jnp.zeros((capacity, doc_rows, doc_rows), jnp.float32)
    )


def shards(counts, block_ids, live_slots, lengths, pairs, pair_count):
    block_count, slot_count, doc_rows, term_columns = counts.shape
    covered_blocks = V // term_columns // lax.axis_size("term")
    local_ids = block_ids - lax.axis_index("term") * covered_blocks
    present = (counts > 0) & (live_slots[:, :, None, None] > 0)
    col_docs = jnp.sum(present.astype(jnp.float32), axis=2)
    freq_part = (
        jnp.zeros((covered_blocks, term_columns), jnp.float32)
        .at[local_ids.reshape(-1)]
        .add(col_docs.reshape(-1, term_columns))
    )
    len_float = lengths.astype(jnp.float32)
    doc_freq, len_total = (
        lax.psum(freq_part.astype(jnp.bfloat16), "doc").astype(jnp.float32),
        lax.psum(jnp.sum(len_float).astype(jnp.bfloat16), "doc").astype(jnp.float32),
    )
    docs_all = len_float.shape[0] * lax.axis_size("doc")
    avg_len = len_total / docs_all
    inv_freq = jnp.log(1.0 + (docs_all - doc_freq + 0.5) / (doc_freq + 0.5))
    slot_freq = inv_freq[local_ids]
    len_scale = (
        1.0
        - length_weight
        + length_weight * len_float.reshape(block_count, 1, doc_rows, 1) / avg_len
    )
    term_freq = counts.astype(jnp.float32)
    weight = jnp.where(
        present,
        slot_freq[:, :, None, :]
        * term_freq
        * (saturation + 1.0)
        / (term_freq + saturation * len_scale),
        0.0,
    )
    square_sum = lax.psum(jnp.sum(weight * weight, axis=(1, 3)), "term")
    normalized = (weight * lax.rsqrt(square_sum + epsilon)[:, None, :, None]).astype(jnp.bfloat16)
    whole_tiles, whole_ids = (
        lax.all_gather(normalized, "doc", axis=0, tiled=True),
        lax.all_gather(block_ids, "doc", axis=0, tiled=True),
    )
    left_base = lax.axis_index("doc") * block_count
    own_count = pair_count[0]
    partial_value = run_pairs(
        pairs, own_count, normalized, block_ids, whole_tiles, whole_ids, left_base
    )
    own_grams = lax.psum_scatter(partial_value, "term", scatter_dimension=1, tiled=True)
    return own_grams


def solution(mesh):
    in_specs = (
        P("doc", "term", None, None),
        P("doc", "term"),
        P("doc", "term"),
        P("doc"),
        P(("doc", "pair"), None),
        P(("doc", "pair")),
    )
    out_specs = P(("doc", "pair"), "term", None)
    return jax.shard_map(shards, mesh=mesh, in_specs=in_specs, out_specs=out_specs, check_vma=False)
```

profile of v0, /device:TPU:1, one launch (start us, length us, event | category | flops | bytes accessed | tf_op | source)
XLA Modules:
  0.0 361.6 jit_solution(16410767193192183070)
XLA Ops:
  6.5 0.7 broadcast_compare_fusion
  7.3 0.7 compare_select_fusion.2
  8.0 0.1 reshape.67
  8.1 1.2 convert_reduce_fusion
  9.2 0.9 scatter_custom_fusion
  10.1 0.8 convert_element_type.29
  11.0 0.0 all-reduce.2.cloned.1.call-update
  11.0 0.0 all-gather.3.cloned.1.call-start
  11.1 1.4 convert_reduce_fusion.1
  12.4 0.1 reshape.103
  12.5 65.9 %psum.22 = bf16[]{:T(256)} all-reduce(bf16[]{:T(256)} %convert_reduce_fusion.1), channel_id=1, replica_groups=mesh['doc'=32,'term'=4,'pair'=2] {'doc'}, use_global_device_ids=true, to_apply=%region_4.0 | all-reduce | flops 1 | bytes 4 | tf_op jit(solution)/shard_map/psum | solution.py:61
  79.1 0.7 multiply_bitcast_fusion
  79.8 49.5 %all-reduce.2.cloned.1.call-done = bf16[2048,128]{1,0:T(8,128)(2,1)} async-done(((bf16[2048,128]{1,0:T(8,128)(2,1)}), bf16[2048,128]{1,0:T(8,128)(2,1)}) %all-reduce.2.cloned.1.call-update) | async-done | bytes 524304 | tf_op jit(solution)/shard_map/psum | solution.py:60
  129.3 1.3 fusion.12
  130.7 0.6 gather_fusion.4
  131.2 0.4 multiply_reduce_fusion
  131.6 9.9 %psum.23 = f32[2,128]{1,0:T(2,128)S(1)} all-reduce(f32[2,128]{1,0:T(2,128)S(1)} %multiply_reduce_fusion), channel_id=1, replica_groups=mesh['doc'=32,'term'=4,'pair'=2] {'term'}, use_global_device_ids=true, to_apply=%region_6.7 | all-reduce | flops 256 | bytes 2048 | tf_op jit(solution)/shard_map/psum | solution.py:81
  141.5 1.0 multiply_convert_fusion
  142.6 0.0 reduce-scatter.2.cloned.1.call-start
  143.3 27.2 %all-gather = s32[32,2,4]{2,1,0:T(2,128)S(1)} all-gather(s32[1,2,4]{2,1,0:T(2,128)S(1)} %bitcast.35), channel_id=1, replica_groups=mesh['doc'=32,'term'=4,'pair'=2] {'doc'}, dimensions={0}, use_global_device_ids=true | all-gather | bytes 1056 | tf_op jit(solution)/shard_map/all_gather | solution.py:85
  170.6 29.1 %all-gather.3.cloned.1.call-done = bf16[64,4,128,128]{3,2,1,0:T(8,128)(2,1)} async-done(((bf16[2,4,128,128]{3,2,1,0:T(8,128)(2,1)}), bf16[64,4,128,128]{3,2,1,0:T(8,128)(2,1)}) %all-gather.3.cloned.1.call-update) | async-done | bytes 8388624 | tf_op jit(solution)/shard_map/all_gather | solution.py:84
  199.7 2.5 broadcast_in_dim.18
  202.2 9.1 %while.10 = (s32[]{:T(128)}, f32[64,128,128]{2,1,0:T(8,128)}, s32[]{:T(128)}, s32[]{:T(128)}, s32[64,2]{0,1:T(2,128)S(1)}, /*index=5*/s32[]{:T(128)}, bf16[2,4,1...) while((s32[]{:T(128)}, f32[64,128,128]{2,1,0:T(8,128)}, ...), condition=%wide.region_8.9_spmd, body=%wide.region_7.8_spmd.sunk | while | flops 138545360 | bytes 8922519 | solution.py:42
  202.2 0.7 add_compare_fusion.2
  202.8 0.1 constant_dynamic-slice_fusion.2
  202.9 0.6 gather_fusion.3
  203.5 0.6 gather_fusion.2
  204.1 4.1 %gather_fusion.1 = bf16[8,4,128,128]{3,2,1,0:T(8,128)(2,1)S(1)} fusion(bf16[64,4,128,128]{3,2,1,0:T(8,128)(2,1)} %get-tuple-element.192, s32[1024]{0:T(1024)S(1)} %get-tuple-element.154), kind=kCustom, calls=%fused_computation.3.clone.1 | custom fusion | bytes 2097184 | tf_op jit(solution)/shard_map/while/body/gather | solution.py:17
  208.2 1.0 fusion.27
  209.2 0.7 gather_fusion
  209.9 1.3 fusion.28
  211.3 143.8 %reduce-scatter.2.cloned.1.call-done = f32[64,32,128]{2,1,0:T(8,128)} async-done(((f32[64,128,128]{2,1,0:T(8,128)}), f32[64,32,128]{2,1,0:T(8,128)}) %reduce-scatter.2.cloned.1.call-update) | async-done | bytes 1048592 | tf_op jit(solution)/shard_map/reduce_scatter | solution.py:92
  (16 shorter events, 0.1 us)
Async XLA Ops:
  6.5 136.8 %copy-start.1 = (s32[2,4]{1,0:T(2,128)S(1)}, s32[2,4]{1,0:T(2,128)}, u32[]{:S(2)}) copy-start(s32[2,4]{1,0:T(2,128)} %param.9) | copy-start | bytes 100
  6.5 124.7 %copy-start.2 = (s32[2,4,128,128]{3,2,1,0:T(8,128)S(1)}, s32[2,4,128,128]{3,2,1,0:T(8,128)}, u32[]{:S(2)}) copy-start(s32[2,4,128,128]{3,2,1,0:T(8,128)} %param.8) | copy-start | bytes 1572868
  6.5 122.8 %all-reduce.2.cloned.1.call-start = ((), (), s32[]{:S(2)}) async-start(), calls=%async_computation.1 | async-start | bytes 1048576 | tf_op jit(solution)/shard_map/psum | solution.py:60
  11.0 191.2 %copy-start.3 = (s32[64,2]{0,1:T(2,128)S(1)}, s32[64,2]{0,1:T(2,128)}, u32[]{:S(2)}) copy-start(s32[64,2]{0,1:T(2,128)} %param.12) | copy-start | bytes 1540
  11.0 188.7 %all-gather.3.cloned.1.call-start = ((), (), s32[]{:S(2)}) async-start(), calls=%async_computation.2 | async-start | bytes 8650752 | tf_op jit(solution)/shard_map/all_gather | solution.py:84
  142.6 59.6 %copy-start = (bf16[2,4,128,128]{3,2,1,0:T(8,128)(2,1)S(1)}, bf16[2,4,128,128]{3,2,1,0:T(8,128)(2,1)}, u32[]{:S(2)}) copy-start(bf16[2,4,128,128]{3,2,1,0:T(8,128)(2,1)} %multiply_convert_fusion) | copy-start | bytes 786436
  142.6 212.5 %reduce-scatter.2.cloned.1.call-start = ((), (), s32[]{:S(2)}) async-start(), calls=%async_computation.3 | async-start | bytes 5242880 | tf_op jit(solution)/shard_map/reduce_scatter | solution.py:92
Sparse Core Ops, SparseCore 0:
  11.1 118.1 all-reduce.1
  142.7 56.9 all-gather.2
  211.4 143.6 reduce-scatter.1
where the time goes:
time: 362 us
  waiting for transfers between devices  222 us (61%)
  blocking collectives  103 us (28%)
  between operations  14.5 us (4%)
  other arithmetic  9.83 us (3%)
  local copies, waits for them, and re-layouts  9.29 us (3%)
    reduce_scatter x1, waiting for transfers between devices, shards(): lax.psum_scatter(partial_value, 'term', scatter_dimension=1, tiled=True)  144 us
    psum x1, blocking collectives, shards(): lax.psum(jnp.sum(len_float).astype(jnp.bfloat16), 'doc').astype(jnp.float32)  65.9 us
    psum x1, waiting for transfers between devices, shards(): lax.psum(freq_part.astype(jnp.bfloat16), 'doc').astype(jnp.float32)  49.5 us
    all_gather x1, waiting for transfers between devices, shards(): lax.all_gather(normalized, 'doc', axis=0, tiled=True)  29.1 us
    all_gather x1, blocking collectives, shards(): lax.all_gather(block_ids, 'doc', axis=0, tiled=True)  27.2 us
    psum x1, blocking collectives, shards(): square_sum = lax.psum(jnp.sum(weight * weight, axis=(1, 3)), 'term')  9.88 us
  transfers between devices with their start and end apart: 3, of which 3 were waited for; matrix products, arithmetic and copies ran while one was open for 1% of the time, Pallas kernels for 0%

commit v1 on v0

--- a/solution.py
+++ b/solution.py
@@ -57,7 +57,7 @@
     )
     len_float = lengths.astype(jnp.float32)
     doc_freq, len_total = (
-        lax.psum(freq_part.astype(jnp.bfloat16), "doc").astype(jnp.float32),
+        jnp.sum(lax.all_gather(freq_part.astype(jnp.bfloat16), "doc"), axis=0).astype(jnp.float32),
         lax.psum(jnp.sum(len_float).astype(jnp.bfloat16), "doc").astype(jnp.float32),
     )
     docs_all = len_float.shape[0] * lax.axis_size("doc")

time: 362 us -> 333 us (0.920)
  waiting for transfers between devices: 222 us -> 186 us
  other arithmetic: 9.83 us -> 17.4 us
    psum x1 -> x0, waiting for transfers between devices: 49.5 us -> none  [shards(): lax.psum(freq_part.astype(jnp.bfloat16), 'doc').astype(jnp.float32)]
    all_gather x0 -> x1, waiting for transfers between devices: none -> 12.4 us  [shards(): lax.all_gather(freq_part.astype(jnp.bfloat16), 'doc')]
    reduce_sum x0 -> x1, other arithmetic: none -> 8.78 us  [shards(): jnp.sum(lax.all_gather(freq_part.astype(jnp.bfloat16), 'doc'), axis=0)]
where the time goes in v1:
time: 333 us
  waiting for transfers between devices  186 us (56%)
  blocking collectives  103 us (31%)
  other arithmetic  17.4 us (5%)
  between operations  14.4 us (4%)
  local copies, waits for them, and re-layouts  9.29 us (3%)
    reduce_scatter x1, waiting for transfers between devices, shards(): lax.psum_scatter(partial_value, 'term', scatter_dimension=1, tiled=True)  144 us
    psum x1, blocking collectives, shards(): lax.psum(jnp.sum(len_float).astype(jnp.bfloat16), 'doc').astype(jnp.float32)  67.1 us
    all_gather x1, waiting for transfers between devices, shards(): lax.all_gather(normalized, 'doc', axis=0, tiled=True)  30.1 us
    all_gather x1, blocking collectives, shards(): lax.all_gather(block_ids, 'doc', axis=0, tiled=True)  25.7 us
    all_gather x1, waiting for transfers between devices, shards(): lax.all_gather(freq_part.astype(jnp.bfloat16), 'doc')  12.4 us
    psum x1, blocking collectives, shards(): square_sum = lax.psum(jnp.sum(weight * weight, axis=(1, 3)), 'term')  9.88 us
    reduce_sum x1, other arithmetic, shards(): jnp.sum(lax.all_gather(freq_part.astype(jnp.bfloat16), 'doc'), axis=0)  8.78 us
  transfers between devices with their start and end apart: 3, of which 3 were waited for; matrix products, arithmetic and copies ran while one was open for 1% of the time, Pallas kernels for 0%

profile of v1, /device:TPU:1, one launch (start us, length us, event | category | flops | bytes accessed | tf_op | source)
XLA Modules:
  0.0 332.6 jit_solution(5367118791989101572)
XLA Ops:
  6.5 0.7 broadcast_compare_fusion
  7.2 0.7 compare_select_fusion.2
  7.9 0.1 reshape.67
  8.0 1.2 convert_reduce_fusion
  9.2 0.9 scatter_custom_fusion
  10.1 0.8 convert_element_type.31
  10.9 0.0 all-gather.5.cloned.1.call-start
  11.0 1.3 convert_reduce_fusion.1
  12.3 67.1 %psum.14 = bf16[]{:T(256)} all-reduce(bf16[]{:T(256)} %convert_reduce_fusion.1), channel_id=1, replica_groups=mesh['doc'=32,'term'=4,'pair'=2] {'doc'}, use_global_device_ids=true, to_apply=%region_4.0 | all-reduce | flops 1 | bytes 4 | tf_op jit(solution)/shard_map/psum | solution.py:61
  79.4 0.1 reshape.103
  80.1 0.7 multiply_bitcast_fusion
  80.8 12.4 %all-gather.7.cloned.1.call-done = bf16[65536,128]{1,0:T(8,128)(2,1)} async-done(((bf16[2048,128]{1,0:T(8,128)(2,1)}), bf16[65536,128]{1,0:T(8,128)(2,1)}) %all-gather.7.cloned.1.call-update) | async-done | bytes 16777232 | tf_op jit(solution)/shard_map/all_gather | solution.py:60
  93.2 8.8 %reduce_sum.40 = bf16[2048,128]{1,0:T(8,128)(2,1)S(1)} reduce(bf16[32,2048,128]{2,1,0:T(8,128)(2,1)} %bitcast.37, bf16[]{:T(256)} %constant.25.clone.1), dimensions={0}, to_apply=%region_2.0 | reduce | flops 8126464 | bytes 17301506 | tf_op jit(solution)/shard_map/reduce_sum | solution.py:60
  102.0 0.3 fusion.12
  102.2 0.6 gather_fusion.4
  102.8 0.4 multiply_reduce_fusion
  103.2 9.9 %psum.15 = f32[2,128]{1,0:T(2,128)S(1)} all-reduce(f32[2,128]{1,0:T(2,128)S(1)} %multiply_reduce_fusion), channel_id=1, replica_groups=mesh['doc'=32,'term'=4,'pair'=2] {'term'}, use_global_device_ids=true, to_apply=%region_6.7 | all-reduce | flops 256 | bytes 2048 | tf_op jit(solution)/shard_map/psum | solution.py:81
  113.1 1.0 multiply_convert_fusion
  114.1 0.0 reduce-scatter.2.cloned.1.call-start
  114.9 25.7 %all-gather.1 = s32[32,2,4]{2,1,0:T(2,128)S(1)} all-gather(s32[1,2,4]{2,1,0:T(2,128)S(1)} %bitcast.36), channel_id=1, replica_groups=mesh['doc'=32,'term'=4,'pair'=2] {'doc'}, dimensions={0}, use_global_device_ids=true | all-gather | bytes 1056 | tf_op jit(solution)/shard_map/all_gather | solution.py:85
  140.6 30.1 %all-gather.5.cloned.1.call-done = bf16[64,4,128,128]{3,2,1,0:T(8,128)(2,1)} async-done(((bf16[2,4,128,128]{3,2,1,0:T(8,128)(2,1)}), bf16[64,4,128,128]{3,2,1,0:T(8,128)(2,1)}) %all-gather.5.cloned.1.call-update) | async-done | bytes 8388624 | tf_op jit(solution)/shard_map/all_gather | solution.py:84
  170.7 2.5 broadcast_in_dim.18
  173.2 9.0 %while.10 = (s32[]{:T(128)}, f32[64,128,128]{2,1,0:T(8,128)}, s32[]{:T(128)}, s32[]{:T(128)}, s32[64,2]{0,1:T(2,128)S(1)}, /*index=5*/s32[]{:T(128)}, bf16[2,4,1...) while((s32[]{:T(128)}, f32[64,128,128]{2,1,0:T(8,128)}, ...), condition=%wide.region_8.9_spmd, body=%wide.region_7.8_spmd.sunk | while | flops 139069648 | bytes 8922519 | solution.py:42
  173.2 0.7 add_compare_fusion.2
  173.9 0.1 constant_dynamic-slice_fusion.2
  174.0 0.6 gather_fusion.3
  174.5 0.6 gather_fusion.2
  175.1 4.1 %gather_fusion.1 = bf16[8,4,128,128]{3,2,1,0:T(8,128)(2,1)S(1)} fusion(bf16[64,4,128,128]{3,2,1,0:T(8,128)(2,1)} %get-tuple-element.192, s32[1024]{0:T(1024)S(1)} %get-tuple-element.154), kind=kCustom, calls=%fused_computation.3.clone.1 | custom fusion | bytes 2097184 | tf_op jit(solution)/shard_map/while/body/gather | solution.py:17
  179.2 1.0 convolution_convert_fusion.2
  180.2 0.7 gather_fusion
  180.9 1.3 fusion.28
  182.3 143.8 %reduce-scatter.2.cloned.1.call-done = f32[64,32,128]{2,1,0:T(8,128)} async-done(((f32[64,128,128]{2,1,0:T(8,128)}), f32[64,32,128]{2,1,0:T(8,128)}) %reduce-scatter.2.cloned.1.call-update) | async-done | bytes 1048592 | tf_op jit(solution)/shard_map/reduce_scatter | solution.py:92
  (17 shorter events, 0.1 us)
Async XLA Ops:
  6.5 86.6 %all-gather.7.cloned.1.call-start = ((), (), s32[]{:S(2)}) async-start(), calls=%async_computation.3 | async-start | bytes 17301504 | tf_op jit(solution)/shard_map/all_gather | solution.py:60
  10.9 159.8 %all-gather.5.cloned.1.call-start = ((), (), s32[]{:S(2)}) async-start(), calls=%async_computation.1 | async-start | bytes 8650752 | tf_op jit(solution)/shard_map/all_gather | solution.py:84
  93.2 9.7 %copy-start.2 = (s32[2,4,128,128]{3,2,1,0:T(8,128)S(1)}, s32[2,4,128,128]{3,2,1,0:T(8,128)}, u32[]{:S(2)}) copy-start(s32[2,4,128,128]{3,2,1,0:T(8,128)} %param.8) | copy-start | bytes 1572868
  93.2 21.7 %copy-start.1 = (s32[2,4]{1,0:T(2,128)S(1)}, s32[2,4]{1,0:T(2,128)}, u32[]{:S(2)}) copy-start(s32[2,4]{1,0:T(2,128)} %param.9) | copy-start | bytes 100
  101.9 71.3 %copy-start.3 = (s32[64,2]{0,1:T(2,128)S(1)}, s32[64,2]{0,1:T(2,128)}, u32[]{:S(2)}) copy-start(s32[64,2]{0,1:T(2,128)} %param.12) | copy-start | bytes 1540
  114.1 59.1 %copy-start = (bf16[2,4,128,128]{3,2,1,0:T(8,128)(2,1)S(1)}, bf16[2,4,128,128]{3,2,1,0:T(8,128)(2,1)}, u32[]{:S(2)}) copy-start(bf16[2,4,128,128]{3,2,1,0:T(8,128)(2,1)} %multiply_convert_fusion) | copy-start | bytes 786436
  114.1 211.9 %reduce-scatter.2.cloned.1.call-start = ((), (), s32[]{:S(2)}) async-start(), calls=%async_computation.2 | async-start | bytes 5242880 | tf_op jit(solution)/shard_map/reduce_scatter | solution.py:92
Sparse Core Ops, SparseCore 0:
  11.1 82.0 all-gather.6
  114.3 56.3 all-gather.4
  182.4 143.6 reduce-scatter.1
